TPU v7x, 512 devices: a whole 4x8x8 slice. The times are simulated.
512 devices in a mesh: gz: 8 (over x, z_lo), row: 8 (over z_hi, core), col: 8 (over y).
Axes of the slice: x: 4, y: 8, z: 8 (z_hi: 4, z_lo: 2; z = z_hi * 2 + z_lo), core: 2. Of those that a mesh axis runs over, the one named last changes fastest.
Arguments:
- front: float32 [4096, 4096], P('row', 'col'), may hold values from -0.04 to 1.45
- lower_parts: float32 [8, 4096, 256], P('gz', 'row'), may hold values from -0.1875 to 0.1875
- upper_parts: float32 [8, 256, 4096], P('gz', None, 'col'), may hold values from -0.125 to 0.125
- pattern: int32 [8, 32, 2], P('gz', 'row'), may hold values 0 or 1
- row_perm: int32 [8, 512], P('row'), may hold values from 0 to 511, as said below
Outputs:
- factored: float32 [4096, 4096], P('row', 'col')
Inputs may be any that keep to these rules, and one draw needn't show every extreme that they name: `row_perm`: each of the 8 rows holds every number 0 to 511 once.
All inputs are finite; a program needn't handle non-finite values. No bound on the sum of `pattern` on one device may be relied on, other than what follows from the above.
Results may differ from a plain program's by a relative error of at most 0.0001.
Values sent between devices are 32-bit elements; how exact they have to be, the bound alone decides.
A program may use at most 64 MiB of HBM per device.

v0:
```python
import jax
import jax.numpy as jnp
from jax import lax
from jax.sharding import PartitionSpec as P

BS = 128
NS_STEPS = 3
PANELS = 2
precise = lax.Precision.HIGHEST


def spread(value, axis, root):
    mine = lax.axis_index(axis) == root
    return lax.psum(jnp.where(mine, value, jnp.zeros_like(value)), axis)


def product(first_matrix, second_matrix):
    return jnp.dot(
        first_matrix, second_matrix, precision=precise, preferred_element_type=jnp.float32
    )


def advance_rows(own_rows, pivot_block, full_inverse):
    return 2.0 * own_rows - product(product(own_rows, pivot_block), full_inverse)


def newton_inverse(pivot_block):
    block_width = pivot_block.shape[0]
    full_inverse = 2.0 * jnp.eye(block_width, dtype=jnp.float32) - pivot_block
    for iteration in range(NS_STEPS - 1):
        full_inverse = advance_rows(full_inverse, pivot_block, full_inverse)
    return full_inverse


def on_device(front, lower_parts, upper_parts, pattern, row_perm):
    panel_width = row_perm.shape[1]
    local_rows, local_cols = front.shape
    blocks_down = local_rows // panel_width
    blocks_across = local_cols // panel_width
    inner_cols = lower_parts.shape[2]
    masked = lower_parts[0].reshape(local_rows // BS, BS, inner_cols // BS, BS)
    masked = masked * pattern[0].astype(jnp.float32)[:, None, :, None]
    partial_value = product(masked.reshape(local_rows, inner_cols), upper_parts[0])
    merged = front - lax.psum(partial_value, "gz")
    sources = (jnp.arange(blocks_down, dtype=jnp.int32) * panel_width)[:, None] + row_perm
    factored = jnp.take(merged, sources.reshape(local_rows), axis=0)
    grid_row = lax.axis_index("row")
    grid_col = lax.axis_index("col")
    row_panels = grid_row * blocks_down + jnp.arange(local_rows, dtype=jnp.int32) // panel_width
    col_panels = grid_col * blocks_across + jnp.arange(local_cols, dtype=jnp.int32) // panel_width
    identity = jnp.eye(panel_width, dtype=jnp.float32)
    for panel_index in range(PANELS):
        owner_row = panel_index // blocks_down
        owner_col = panel_index // blocks_across
        row_start = panel_index % blocks_down * panel_width
        col_start = panel_index % blocks_across * panel_width
        panel_row = spread(factored, "row", owner_row)
        in_column = grid_col == owner_col
        pivot_block = jnp.where(in_column, panel_row, identity)
        inverse = newton_inverse(pivot_block)
        column_block = factored
        lower_own = product(column_block, inverse)
        lower_recv = spread(lower_own, "col", owner_col)
        below_rows = row_panels > panel_index
        trailing = below_rows[:, None] & (col_panels > panel_index)[None, :]
        factored = factored - jnp.where(trailing, product(lower_recv, panel_row), 0.0)
        current = factored
        stacked = jnp.tile(inverse, (blocks_down, 1))
        diagonal_rows = row_panels == panel_index
        replaced = jnp.where(
            below_rows[:, None], lower_own, jnp.where(diagonal_rows[:, None], stacked, current)
        )
        factored = factored.at[:, col_start : col_start + panel_width].set(
            jnp.where(in_column, replaced, current)
        )
    return factored


def solution(mesh):
    in_specs = (
        P("row", "col"),
        P("gz", "row", None),
        P("gz", None, "col"),
        P("gz", "row", None),
        P("row", None),
    )
    out_specs = P("row", "col")
    return jax.shard_map(
        on_device, mesh=mesh, in_specs=in_specs, out_specs=out_specs, check_vma=False
    )
```

profile of v0, /device:TPU:2, one launch (start us, length us, event | category | flops | bytes accessed | tf_op | source)
XLA Modules:
  0.0 472.1 jit_solution(3480206786806552087)
XLA Ops:
  6.5 0.7 convert_bitcast_fusion
  8.0 0.6 copy-done.6
  8.6 2.0 fusion.10
  10.7 0.7 copy-done.7
  11.5 92.9 %all-reduce.6.cloned.1.call-done = f32[512,512]{1,0:T(8,128)} async-done(((f32[512,512]{1,0:T(8,128)}), f32[512,512]{1,0:T(8,128)}) %all-reduce.6.cloned.1.call-update) | async-done | bytes 1048592 | tf_op jit(solution)/shard_map/psum | solution.py:44
  104.4 1.4 sub.38
  105.9 1.6 gather_fusion
  107.5 1.1 select_select_fusion.2
  108.7 83.7 %all-reduce.8.cloned.1.call-done = f32[512,512]{1,0:T(8,128)} async-done(((f32[512,512]{1,0:T(8,128)}), f32[512,512]{1,0:T(8,128)}) %all-reduce.8.cloned.1.call-update) | async-done | bytes 1048592 | tf_op jit(solution)/shard_map/psum | solution.py:14
  192.4 3.6 fusion.2
  196.0 1.9 convolution_subtract_fusion.3
  197.9 1.9 fusion.8
  199.8 1.9 convolution_subtract_fusion.2
  201.7 3.2 broadcast_select_fusion.2
  205.2 77.8 %all-reduce.10.cloned.1.call-done = f32[512,512]{1,0:T(8,128)} async-done(((f32[512,512]{1,0:T(8,128)}), f32[512,512]{1,0:T(8,128)}) %all-reduce.10.cloned.1.call-update) | async-done | bytes 1048592 | tf_op jit(solution)/shard_map/psum | solution.py:14
  283.0 5.2 %broadcast_select_fusion.1 = (f32[512,512]{1,0:T(8,128)}, f32[512,512]{1,0:T(8,128)}) fusion(pred[]{:T(512)S(6)} %eq.44, f32[512,512]{1,0:T(8,128)} %get-tuple-element.46, f32[512,512]{1,0:T(8,128)} %copy-done.3, f32[512,512]{1,0:T(8,128)} %all-reduce.10.cloned.1.call-done, f32[512,512]{1,0:T(8,128)S(1)} %copy-done.1, pred[512]{0:T(512)(128)(4,1)S(1)} %fusion.36, ...), kind=kOutput, calls=%fused_computation.32 | convolution fusion | flops 1612709888 | bytes 7342082 | tf_op jit(solution)/shard_map/dot_general | solution.py:18
  288.3 81.9 %all-reduce.12.cloned.1.call-done = f32[512,512]{1,0:T(8,128)} async-done(((f32[512,512]{1,0:T(8,128)}), f32[512,512]{1,0:T(8,128)}) %all-reduce.12.cloned.1.call-update) | async-done | bytes 1048592 | tf_op jit(solution)/shard_map/psum | solution.py:14
  370.2 2.0 fusion.4
  372.2 1.9 convolution_subtract_fusion.1
  374.1 1.9 fusion.9
  376.0 1.8 convolution_subtract_fusion
  377.9 3.2 broadcast_select_fusion
  381.1 79.7 %all-reduce.14.cloned.1.call-done = f32[512,512]{1,0:T(8,128)} async-done(((f32[512,512]{1,0:T(8,128)}), f32[512,512]{1,0:T(8,128)}) %all-reduce.14.cloned.1.call-update) | async-done | bytes 1048592 | tf_op jit(solution)/shard_map/psum | solution.py:14
  460.8 4.8 %select_select_fusion = f32[512,512]{1,0:T(8,128)} fusion(f32[512,512]{1,0:T(8,128)} %get-tuple-element.50, f32[512,512]{1,0:T(8,128)S(1)} %convolution_subtract_fusion, f32[512,512]{1,0:T(8,128)} %get-tuple-element.48, f32[512,512]{1,0:T(8,128)} %all-reduce.14.cloned.1.call-done, f32[512,512]{1,0:T(8,128)S(1)} %copy-done.2, ...), kind=kOutput, calls=%fused_computation.17 | convolution fusion | flops 1612185600 | bytes 6292993 | tf_op jit(solution)/shard_map/dot_general | solution.py:18
  (34 shorter events, 1.2 us)
Async XLA Ops:
  6.5 1.5 copy-start
  6.5 97.9 %all-reduce.6.cloned.1.call-start = ((), (), s32[]{:S(2)}) async-start(), calls=%async_computation | async-start | bytes 2097152 | tf_op jit(solution)/shard_map/psum | solution.py:44
  7.6 1.0 copy-start.6
  10.6 93.8 %copy-start.5 = (f32[512,512]{1,0:T(8,128)S(1)}, f32[512,512]{1,0:T(8,128)}, u32[]{:S(2)}) copy-start(f32[512,512]{1,0:T(8,128)} %param.13) | copy-start | bytes 3145732
  10.7 181.7 %all-reduce.8.cloned.1.call-start = ((), (), s32[]{:S(2)}) async-start(), calls=%async_computation.1 | async-start | bytes 2097152 | tf_op jit(solution)/shard_map/psum | solution.py:14
  10.7 0.8 copy-start.7
  108.7 174.4 %all-reduce.10.cloned.1.call-start = ((), (), s32[]{:S(2)}) async-start(), calls=%async_computation.2 | async-start | bytes 2097152 | tf_op jit(solution)/shard_map/psum | solution.py:14
  192.4 3.6 copy-start.1
  201.7 3.2 copy-start.3
  205.0 165.3 %all-reduce.12.cloned.1.call-start = ((), (), s32[]{:S(2)}) async-start(), calls=%async_computation.3 | async-start | bytes 2097152 | tf_op jit(solution)/shard_map/psum | solution.py:14
  288.3 172.5 %all-reduce.14.cloned.1.call-start = ((), (), s32[]{:S(2)}) async-start(), calls=%async_computation.4 | async-start | bytes 2097152 | tf_op jit(solution)/shard_map/psum | solution.py:14
  370.2 2.0 copy-start.2
  376.0 1.9 copy-start.4
Sparse Core Ops, SparseCore 0:
  10.8 93.6 all-reduce.5
  108.8 83.5 all-reduce.7
  205.1 77.9 all-reduce.9
  288.4 81.7 all-reduce.11
  381.2 79.5 all-reduce.13
where the time goes:
time: 472 us
  waiting for transfers between devices  416 us (88%)
  matrix products  35.3 us (7%)
  between operations  13.4 us (3%)
    psum x4, waiting for transfers between devices, spread(): return lax.psum(jnp.where(mine, value, jnp.zeros_like(value)), axis)  323 us
    psum x1, waiting for transfers between devices, on_device(): merged = front - lax.psum(partial_value, 'gz')  92.9 us
    dot_general x13, matrix products, product(): jnp.dot(first_matrix, second_matrix, precision=precise, preferred_element...  35.3 us
  transfers between devices with their start and end apart: 5, of which 5 were waited for; matrix products, arithmetic and copies ran while one was open for 0% of the time, Pallas kernels for 0%

commit v1 on v0

--- a/solution.py
+++ b/solution.py
@@ -9,9 +9,14 @@
 precise = lax.Precision.HIGHEST
 
 
+def fix_values(local_values, axis_tag):
+    y1 = jnp.sum(lax.all_gather(local_values, axis_tag), axis=0)
+    return y1
+
+
 def spread(value, axis, root):
     mine = lax.axis_index(axis) == root
-    return lax.psum(jnp.where(mine, value, jnp.zeros_like(value)), axis)
+    return fix_values(jnp.where(mine, value, jnp.zeros_like(value)), axis)
 
 
 def product(first_matrix, second_matrix):

time: 472 us -> 541 us (1.15)
  the two profiles are of different devices: /device:TPU:2 before, /device:TPU:1 now
where the time goes in v1:
time: 541 us
  waiting for transfers between devices  464 us (86%)
  matrix products  34.7 us (6%)
  other arithmetic  24.9 us (5%)
  between operations  13.3 us (2%)
    all_gather x4, waiting for transfers between devices, fix_values(): y1 = jnp.sum(lax.all_gather(local_values, axis_tag), axis=0)  373 us
    psum x1, waiting for transfers between devices, on_device(): merged = front - lax.psum(partial_value, 'gz')  90.8 us
    dot_general x13, matrix products, product(): jnp.dot(first_matrix, second_matrix, precision=precise, preferred_element...  34.7 us
    reduce_sum x4, other arithmetic, fix_values(): y1 = jnp.sum(lax.all_gather(local_values, axis_tag), axis=0)  19.9 us
  transfers between devices with their start and end apart: 5, of which 5 were waited for; matrix products, arithmetic and copies ran while one was open for 0% of the time, Pallas kernels for 0%

profile of v1, /device:TPU:1, one launch (start us, length us, event | category | flops | bytes accessed | tf_op | source)
XLA Modules:
  0.0 540.6 jit_solution(6483370212897114953)
XLA Ops:
  8.0 3.0 fusion.11
  12.5 90.8 %all-reduce.2.cloned.1.call-done = f32[512,512]{1,0:T(8,128)} async-done(((f32[512,512]{1,0:T(8,128)}), f32[512,512]{1,0:T(8,128)}) %all-reduce.2.cloned.1.call-update) | async-done | bytes 1048592 | tf_op jit(solution)/shard_map/psum | solution.py:49
  103.3 1.7 sub.38
  105.1 1.6 gather_fusion
  108.1 94.7 %all-gather.8.cloned.1.call-done = f32[8,512,512]{2,1,0:T(8,128)} async-done(((f32[1,512,512]{2,1,0:T(8,128)}), f32[8,512,512]{2,1,0:T(8,128)}) %all-gather.8.cloned.1.call-update) | async-done | bytes 8388624 | tf_op jit(solution)/shard_map/all_gather | solution.py:13
  202.8 4.5 reduce_sum.36
  207.3 1.9 fusion.2
  209.3 1.9 convolution_subtract_fusion.3
  211.2 1.9 fusion.9
  213.1 1.9 convolution_subtract_fusion.2
  216.0 3.2 broadcast_select_fusion.2
  219.5 93.7 %all-gather.10.cloned.1.call-done = f32[4096,512]{1,0:T(8,128)} async-done(((f32[512,512]{1,0:T(8,128)}), f32[4096,512]{1,0:T(8,128)}) %all-gather.10.cloned.1.call-update) | async-done | bytes 8388624 | tf_op jit(solution)/shard_map/all_gather | solution.py:13
  313.2 5.5 %reduce_sum.37 = f32[512,512]{1,0:T(8,128)} reduce(f32[8,512,512]{2,1,0:T(8,128)} %bitcast.34, f32[]{:T(128)} %constant.130.clone.1), dimensions={0}, to_apply=%region_2.3 | reduce | flops 1835008 | bytes 9437188 | tf_op jit(solution)/shard_map/reduce_sum | solution.py:13
  318.6 5.2 broadcast_select_fusion.1
  323.9 90.6 %all-gather.12.cloned.1.call-done = f32[4096,512]{1,0:T(8,128)} async-done(((f32[512,512]{1,0:T(8,128)}), f32[4096,512]{1,0:T(8,128)}) %all-gather.12.cloned.1.call-update) | async-done | bytes 8388624 | tf_op jit(solution)/shard_map/all_gather | solution.py:13
  414.5 4.5 reduce_sum.38
  419.0 1.9 fusion.4
  421.0 1.9 convolution_subtract_fusion.1
  422.9 1.9 fusion.10
  424.8 1.8 convolution_subtract_fusion
  426.7 3.2 broadcast_select_fusion
  429.9 93.9 %all-gather.14.cloned.1.call-done = f32[4096,512]{1,0:T(8,128)} async-done(((f32[512,512]{1,0:T(8,128)}), f32[4096,512]{1,0:T(8,128)}) %all-gather.14.cloned.1.call-update) | async-done | bytes 8388624 | tf_op jit(solution)/shard_map/all_gather | solution.py:13
  523.8 5.5 %reduce_sum.39 = f32[512,512]{1,0:T(8,128)} reduce(f32[8,512,512]{2,1,0:T(8,128)} %bitcast.35, f32[]{:T(128)} %constant.130.clone.1), dimensions={0}, to_apply=%region_4.5 | reduce | flops 1835008 | bytes 9437188 | tf_op jit(solution)/shard_map/reduce_sum | solution.py:13
  529.3 4.8 select_select_fusion
  (28 shorter events, 5.6 us)
Async XLA Ops:
  6.5 1.5 copy-start
  6.5 96.8 %all-reduce.2.cloned.1.call-start = ((), (), s32[]{:S(2)}) async-start(), calls=%async_computation | async-start | bytes 2097152 | tf_op jit(solution)/shard_map/psum | solution.py:49
  11.1 191.7 %all-gather.8.cloned.1.call-start = ((), (), s32[]{:S(2)}) async-start(), calls=%async_computation.1 | async-start | bytes 9437184 | tf_op jit(solution)/shard_map/all_gather | solution.py:13
  107.9 205.3 %all-gather.10.cloned.1.call-start = ((), (), s32[]{:S(2)}) async-start(), calls=%async_computation.2 | async-start | bytes 9437184 | tf_op jit(solution)/shard_map/all_gather | solution.py:13
  215.0 1.0 copy-start.1
  219.2 195.3 %all-gather.12.cloned.1.call-start = ((), (), s32[]{:S(2)}) async-start(), calls=%async_computation.3 | async-start | bytes 9437184 | tf_op jit(solution)/shard_map/all_gather | solution.py:13
  323.9 199.9 %all-gather.14.cloned.1.call-start = ((), (), s32[]{:S(2)}) async-start(), calls=%async_computation.4 | async-start | bytes 9437184 | tf_op jit(solution)/shard_map/all_gather | solution.py:13
  419.0 7.7 %copy-start.2 = (f32[512,512]{1,0:T(8,128)S(1)}, f32[512,512]{1,0:T(8,128)}, u32[]{:S(2)}) copy-start(f32[512,512]{1,0:T(8,128)} %get-tuple-element.48) | copy-start | bytes 3145732
Sparse Core Ops, SparseCore 0:
  11.2 92.0 all-reduce.1
  108.0 94.7 all-gather.7
  219.3 93.7 all-gather.9
  324.0 90.4 all-gather.11
  430.0 93.7 all-gather.13
